TPU v7x, 32 devices: a whole 2x2x4 slice. The times are simulated.
32 devices in a mesh: param: 16 (over z, y, core), tm: 2 (over x).
Axes of the slice: x: 2, y: 2, z: 4, core: 2. Of those that a mesh axis runs over, the one named last changes fastest.
Arguments:
- params: bfloat16 [32, 32, 8192], P(None, 'tm', 'param'), may hold values from -6 to 6
- kernel: bfloat16 [8, 8192, 600], P(None, 'param'), may hold values from -0.0234375 to 0.0234375
- lag_offsets: int32 [8], replicated, may hold values from 0 to 11, as said below
- observed: bfloat16 [32, 32, 600], P(None, 'tm'), may hold values from -6 to 6
- diag_inverse: float32 [600, 600], replicated, may hold values from -2 to 2, as said below
- coupling: float32 [3, 600, 600], replicated, may hold values from -26 to 26
Outputs:
- whitened: float32 [32, 32, 600], P(None, 'tm')
Inputs may be any that keep to these rules, and one draw needn't show every extreme that they name: `lag_offsets`: the offsets are distinct and one of them is always 12 - 1. `diag_inverse`: lower triangular with a positive diagonal.
All inputs are finite; a program needn't handle non-finite values.
Results may differ from a plain program's by a relative error of at most 0.0003.
Values may be sent and summed in bfloat16 or wider, within the bound.
A program may use at most 64 MiB of HBM per device.

v0:
```python
import jax
import jax.numpy as jnp
from jax import lax
from jax.sharding import PartitionSpec as P

REACH = 12


def from_behind(block, axis, distance):
    devices = range(lax.axis_size(axis))
    route = [(i - distance, i) for i in devices if i - distance in devices]
    return lax.ppermute(block, axis, route)


def solve_block(misfit, incoming, diag_inverse, coupling):

    def advance(history, current):
        balance = current - jnp.einsum(
            "jsn,jmn->sm", history, coupling, precision=lax.Precision.HIGHEST
        )
        solved = jnp.dot(balance, diag_inverse.T, precision=lax.Precision.HIGHEST)
        history = jnp.concatenate([solved[None], history[:-1]], axis=0)
        return (history, solved)

    final_history, solved_all = lax.scan(advance, incoming, jnp.swapaxes(misfit, 0, 1))
    return (jnp.swapaxes(solved_all, 0, 1), final_history)


def per_device(params, kernel, lag_offsets, observed, diag_inverse, coupling):
    samples, step_count, col_count = params.shape
    lag_count, unused_cols, sensors = kernel.shape
    flat_kernel = kernel.reshape(lag_count * col_count, sensors)
    rim = from_behind(params[:, step_count - (REACH - 1) :, :], "tm", 1)
    source = jnp.concatenate([rim, params], axis=1)
    windows = [
        lax.dynamic_slice_in_dim(source, REACH - 1 - lag_offsets[lag_index], step_count, 1)
        for lag_index in range(lag_count)
    ]
    stacked = jnp.stack(windows, axis=2).reshape(samples * step_count, lag_count * col_count)
    product = jnp.dot(stacked, flat_kernel, preferred_element_type=jnp.float32)
    local = product.reshape(samples, step_count, sensors)
    summed = lax.psum_scatter(local, "param", scatter_dimension=0, tiled=True)
    share = summed.shape[0]
    mine = lax.dynamic_slice_in_dim(observed, lax.axis_index("param") * share, share, 0)
    misfit = mine.astype(jnp.float32) - summed
    local_samples = misfit.shape[0]
    position = lax.axis_index("tm")
    state = jnp.zeros((coupling.shape[0], local_samples, sensors), jnp.float32)
    outputs = jnp.zeros_like(misfit)

    def turn(turn_index, carry):
        solved_now, history = carry
        incoming = from_behind(history, "tm", 1)
        return lax.cond(
            position == turn_index,
            lambda: solve_block(misfit, incoming, diag_inverse, coupling),
            lambda: (solved_now, history),
        )

    outputs, state = lax.fori_loop(0, lax.axis_size("tm"), turn, (outputs, state))
    return lax.all_gather(outputs, "param", axis=0, tiled=True)


def solution(mesh):
    in_specs = (P(None, "tm", "param"), P(None, "param", None), P(), P(None, "tm", None), P(), P())
    out_specs = P(None, "tm", None)
    return jax.shard_map(
        per_device, mesh=mesh, in_specs=in_specs, out_specs=out_specs, check_vma=False
    )
```

profile of v0, /device:TPU:0, one launch (start us, length us, event | category | flops | bytes accessed | tf_op | source)
XLA Modules:
  0.0 416.1 jit_solution(11793586352169557992)
XLA Ops:
  7.8 4.9 %collective-permute-start.1 = (bf16[32,11,512]{2,1,0:T(8,128)(2,1)S(1)}, bf16[32,11,512]{2,1,0:T(8,128)(2,1)S(1)}, u32[]{:S(2)}, u32[]{:S(2)}) collective-permute-start(bf16[32,11,512]{2,1,0:T(8,128)(2,1)S(1)} %slice.30), channel_id=1, source_target_pairs={{0,1},{2,3},{4,5},{6,7},{8,9},{10,11},{12,13},{14,15},{16,17},{18,... | collective-permute-start | bytes 1081352 | tf_op jit(solution)/shard_map/ppermute | solution.py:12
  12.7 1.6 fusion.30
  24.7 1.6 fusion.11
  26.3 1.5 fusion.14
  30.4 4.5 %fusion.3 = f32[32,16,600]{2,1,0:T(8,128)} fusion(bf16[32,16,8,512]{3,1,2,0:T(8,128)(2,1)S(1)} %fusion.8, bf16[8,512,600]{1,2,0:T(8,128)(2,1)S(1)} %bitcast.85), kind=kOutput, calls=%fused_computation.23 | convolution fusion | flops 2516582400 | bytes 10338304 | tf_op jit(solution)/shard_map/dot_general | solution.py:40
  35.0 60.1 %reduce-scatter.2.cloned.1.call-done = f32[2,16,600]{2,1,0:T(8,128)} async-done(((f32[32,16,600]{2,1,0:T(8,128)}), f32[2,16,600]{2,1,0:T(8,128)}) %reduce-scatter.2.cloned.1.call-update) | async-done | bytes 76816 | tf_op jit(solution)/shard_map/reduce_scatter | solution.py:42
  96.7 138.7 %while.27 = (s32[]{:T(128)}, f32[2,16,600]{2,0,1:T(2,128)}, f32[3,2,600]{2,1,0:T(2,128)S(1)}, s32[]{:T(128)}, f32[2,16,600]{2,0,1:T(2,128)S(1)}, /*index=5*/f32[...) while((s32[]{:T(128)}, f32[2,16,600]{2,0,1:T(2,128)}, f32[3,2,600]{2,1,0:T(2,128)S(1)}, s32[]{:T(128)}, ...), condition=%wide.region_6.7_spmd, body=%wide.region_1.6_spmd.sunk | while | flops 34564804 | bytes 5933988 | solution.py:60
  96.7 3.4 collective-permute-start
  100.1 1.4 collective-permute-done
  101.5 131.2 %conditional.2 = ((f32[2,16,600]{2,0,1:T(2,128)}, f32[3,2,600]{2,1,0:T(2,128)S(1)})) conditional(s32[]{:T(128)} %convert_element_type.13, (f32[2,16,600]{2,0,1:T(2,128)}, f32[3,2,600]{2,1,0:T(2,128)S(1)}) %tuple.59, (f32[2,16,600]{2,0,1:T(2,128)S(1)}, f32[3,600,600]{2,1,0:T(8,128)}, f32[600,600]{1,0:T(8,128)S(1)}, f32[3,2,600]{2,1,0:T(2,128)S(1)}) %tuple.60), branch_computations={%region_2.0_spmd, %region_3.5_spmd} | conditional | flops 34564800 | bytes 5876201 | solution.py:54
  101.5 131.2 %while.26 = (s32[]{:T(128)}, f32[3,2,600]{2,1,0:T(2,128)S(1)}, f32[16,2,600]{2,1,0:T(2,128)}, f32[16,2,600]{2,1,0:T(2,128)S(1)}, f32[3,600,600]{2,1,0:T(8,128)}, /*index=5*/f32[600,600]{1,0:T(8,128)S(1)}, s32[]{:T(128)}) while((s32[]{:T(128)}, f32[3,2,600]{2,1,0:T(2,128)S(1)}, f32[16,2,600]{2,1,0:T(2,128)}, f32[16,2,600]{2,1,0:T(2,128)S(1)}, ...), condition=%wide.region_5.4_spmd, body=%wide.region_4.3_spmd.sunk | while | flops 34564800 | bytes 5847313 | solution.py:25
  101.5 6.1 %fusion.45 = f32[2,600]{1,0:T(2,128)S(1)} fusion(f32[3,2,600]{2,1,0:T(2,128)S(1)} %get-tuple-element.331, f32[3,600,600]{2,1,0:T(8,128)} %get-tuple-element.341, f32[16,2,600]{2,1,0:T(2,128)S(1)} %get-tuple-element.340, s32[]{:T(128)} %get-tuple-element.330), kind=kOutput, calls=%fused_computation.2.clone.1 | convolution fusion | flops 25921200 | bytes 4344004 | tf_op jit(solution)/shard_map/while/body/eval_jaxpr/cond/branch_1_fun/while/body/eval_jaxpr/jsn,jmn->sm/dot_general | solution.py:18
  107.7 2.0 constant_dynamic-update-slice_fusion.2
  109.7 6.1 %fusion.45 = f32[2,600]{1,0:T(2,128)S(1)} fusion(f32[3,2,600]{2,1,0:T(2,128)S(1)} %get-tuple-element.331, f32[3,600,600]{2,1,0:T(8,128)} %get-tuple-element.341, f32[16,2,600]{2,1,0:T(2,128)S(1)} %get-tuple-element.340, s32[]{:T(128)} %get-tuple-element.330), kind=kOutput, calls=%fused_computation.2.clone.1 | convolution fusion | flops 25921200 | bytes 4344004 | tf_op jit(solution)/shard_map/while/body/eval_jaxpr/cond/branch_1_fun/while/body/eval_jaxpr/jsn,jmn->sm/dot_general | solution.py:18
  115.9 2.0 constant_dynamic-update-slice_fusion.2
  117.9 6.1 %fusion.45 = f32[2,600]{1,0:T(2,128)S(1)} fusion(f32[3,2,600]{2,1,0:T(2,128)S(1)} %get-tuple-element.331, f32[3,600,600]{2,1,0:T(8,128)} %get-tuple-element.341, f32[16,2,600]{2,1,0:T(2,128)S(1)} %get-tuple-element.340, s32[]{:T(128)} %get-tuple-element.330), kind=kOutput, calls=%fused_computation.2.clone.1 | convolution fusion | flops 25921200 | bytes 4344004 | tf_op jit(solution)/shard_map/while/body/eval_jaxpr/cond/branch_1_fun/while/body/eval_jaxpr/jsn,jmn->sm/dot_general | solution.py:18
  124.1 2.0 constant_dynamic-update-slice_fusion.2
  126.1 6.1 %fusion.45 = f32[2,600]{1,0:T(2,128)S(1)} fusion(f32[3,2,600]{2,1,0:T(2,128)S(1)} %get-tuple-element.331, f32[3,600,600]{2,1,0:T(8,128)} %get-tuple-element.341, f32[16,2,600]{2,1,0:T(2,128)S(1)} %get-tuple-element.340, s32[]{:T(128)} %get-tuple-element.330), kind=kOutput, calls=%fused_computation.2.clone.1 | convolution fusion | flops 25921200 | bytes 4344004 | tf_op jit(solution)/shard_map/while/body/eval_jaxpr/cond/branch_1_fun/while/body/eval_jaxpr/jsn,jmn->sm/dot_general | solution.py:18
  132.3 2.0 constant_dynamic-update-slice_fusion.2
  134.3 6.1 %fusion.45 = f32[2,600]{1,0:T(2,128)S(1)} fusion(f32[3,2,600]{2,1,0:T(2,128)S(1)} %get-tuple-element.331, f32[3,600,600]{2,1,0:T(8,128)} %get-tuple-element.341, f32[16,2,600]{2,1,0:T(2,128)S(1)} %get-tuple-element.340, s32[]{:T(128)} %get-tuple-element.330), kind=kOutput, calls=%fused_computation.2.clone.1 | convolution fusion | flops 25921200 | bytes 4344004 | tf_op jit(solution)/shard_map/while/body/eval_jaxpr/cond/branch_1_fun/while/body/eval_jaxpr/jsn,jmn->sm/dot_general | solution.py:18
  140.5 2.0 constant_dynamic-update-slice_fusion.2
  142.5 6.1 %fusion.45 = f32[2,600]{1,0:T(2,128)S(1)} fusion(f32[3,2,600]{2,1,0:T(2,128)S(1)} %get-tuple-element.331, f32[3,600,600]{2,1,0:T(8,128)} %get-tuple-element.341, f32[16,2,600]{2,1,0:T(2,128)S(1)} %get-tuple-element.340, s32[]{:T(128)} %get-tuple-element.330), kind=kOutput, calls=%fused_computation.2.clone.1 | convolution fusion | flops 25921200 | bytes 4344004 | tf_op jit(solution)/shard_map/while/body/eval_jaxpr/cond/branch_1_fun/while/body/eval_jaxpr/jsn,jmn->sm/dot_general | solution.py:18
  148.7 2.0 constant_dynamic-update-slice_fusion.2
  150.7 6.1 %fusion.45 = f32[2,600]{1,0:T(2,128)S(1)} fusion(f32[3,2,600]{2,1,0:T(2,128)S(1)} %get-tuple-element.331, f32[3,600,600]{2,1,0:T(8,128)} %get-tuple-element.341, f32[16,2,600]{2,1,0:T(2,128)S(1)} %get-tuple-element.340, s32[]{:T(128)} %get-tuple-element.330), kind=kOutput, calls=%fused_computation.2.clone.1 | convolution fusion | flops 25921200 | bytes 4344004 | tf_op jit(solution)/shard_map/while/body/eval_jaxpr/cond/branch_1_fun/while/body/eval_jaxpr/jsn,jmn->sm/dot_general | solution.py:18
  156.9 2.0 constant_dynamic-update-slice_fusion.2
  158.9 6.1 %fusion.45 = f32[2,600]{1,0:T(2,128)S(1)} fusion(f32[3,2,600]{2,1,0:T(2,128)S(1)} %get-tuple-element.331, f32[3,600,600]{2,1,0:T(8,128)} %get-tuple-element.341, f32[16,2,600]{2,1,0:T(2,128)S(1)} %get-tuple-element.340, s32[]{:T(128)} %get-tuple-element.330), kind=kOutput, calls=%fused_computation.2.clone.1 | convolution fusion | flops 25921200 | bytes 4344004 | tf_op jit(solution)/shard_map/while/body/eval_jaxpr/cond/branch_1_fun/while/body/eval_jaxpr/jsn,jmn->sm/dot_general | solution.py:18
  165.1 2.0 constant_dynamic-update-slice_fusion.2
  167.1 6.1 %fusion.45 = f32[2,600]{1,0:T(2,128)S(1)} fusion(f32[3,2,600]{2,1,0:T(2,128)S(1)} %get-tuple-element.331, f32[3,600,600]{2,1,0:T(8,128)} %get-tuple-element.341, f32[16,2,600]{2,1,0:T(2,128)S(1)} %get-tuple-element.340, s32[]{:T(128)} %get-tuple-element.330), kind=kOutput, calls=%fused_computation.2.clone.1 | convolution fusion | flops 25921200 | bytes 4344004 | tf_op jit(solution)/shard_map/while/body/eval_jaxpr/cond/branch_1_fun/while/body/eval_jaxpr/jsn,jmn->sm/dot_general | solution.py:18
  173.3 2.0 constant_dynamic-update-slice_fusion.2
  175.3 6.1 %fusion.45 = f32[2,600]{1,0:T(2,128)S(1)} fusion(f32[3,2,600]{2,1,0:T(2,128)S(1)} %get-tuple-element.331, f32[3,600,600]{2,1,0:T(8,128)} %get-tuple-element.341, f32[16,2,600]{2,1,0:T(2,128)S(1)} %get-tuple-element.340, s32[]{:T(128)} %get-tuple-element.330), kind=kOutput, calls=%fused_computation.2.clone.1 | convolution fusion | flops 25921200 | bytes 4344004 | tf_op jit(solution)/shard_map/while/body/eval_jaxpr/cond/branch_1_fun/while/body/eval_jaxpr/jsn,jmn->sm/dot_general | solution.py:18
  181.5 2.0 constant_dynamic-update-slice_fusion.2
  183.5 6.1 %fusion.45 = f32[2,600]{1,0:T(2,128)S(1)} fusion(f32[3,2,600]{2,1,0:T(2,128)S(1)} %get-tuple-element.331, f32[3,600,600]{2,1,0:T(8,128)} %get-tuple-element.341, f32[16,2,600]{2,1,0:T(2,128)S(1)} %get-tuple-element.340, s32[]{:T(128)} %get-tuple-element.330), kind=kOutput, calls=%fused_computation.2.clone.1 | convolution fusion | flops 25921200 | bytes 4344004 | tf_op jit(solution)/shard_map/while/body/eval_jaxpr/cond/branch_1_fun/while/body/eval_jaxpr/jsn,jmn->sm/dot_general | solution.py:18
  189.7 2.0 constant_dynamic-update-slice_fusion.2
  191.7 6.1 %fusion.45 = f32[2,600]{1,0:T(2,128)S(1)} fusion(f32[3,2,600]{2,1,0:T(2,128)S(1)} %get-tuple-element.331, f32[3,600,600]{2,1,0:T(8,128)} %get-tuple-element.341, f32[16,2,600]{2,1,0:T(2,128)S(1)} %get-tuple-element.340, s32[]{:T(128)} %get-tuple-element.330), kind=kOutput, calls=%fused_computation.2.clone.1 | convolution fusion | flops 25921200 | bytes 4344004 | tf_op jit(solution)/shard_map/while/body/eval_jaxpr/cond/branch_1_fun/while/body/eval_jaxpr/jsn,jmn->sm/dot_general | solution.py:18
  197.9 2.0 constant_dynamic-update-slice_fusion.2
  199.9 6.1 %fusion.45 = f32[2,600]{1,0:T(2,128)S(1)} fusion(f32[3,2,600]{2,1,0:T(2,128)S(1)} %get-tuple-element.331, f32[3,600,600]{2,1,0:T(8,128)} %get-tuple-element.341, f32[16,2,600]{2,1,0:T(2,128)S(1)} %get-tuple-element.340, s32[]{:T(128)} %get-tuple-element.330), kind=kOutput, calls=%fused_computation.2.clone.1 | convolution fusion | flops 25921200 | bytes 4344004 | tf_op jit(solution)/shard_map/while/body/eval_jaxpr/cond/branch_1_fun/while/body/eval_jaxpr/jsn,jmn->sm/dot_general | solution.py:18
  206.1 2.0 constant_dynamic-update-slice_fusion.2
  208.1 6.1 %fusion.45 = f32[2,600]{1,0:T(2,128)S(1)} fusion(f32[3,2,600]{2,1,0:T(2,128)S(1)} %get-tuple-element.331, f32[3,600,600]{2,1,0:T(8,128)} %get-tuple-element.341, f32[16,2,600]{2,1,0:T(2,128)S(1)} %get-tuple-element.340, s32[]{:T(128)} %get-tuple-element.330), kind=kOutput, calls=%fused_computation.2.clone.1 | convolution fusion | flops 25921200 | bytes 4344004 | tf_op jit(solution)/shard_map/while/body/eval_jaxpr/cond/branch_1_fun/while/body/eval_jaxpr/jsn,jmn->sm/dot_general | solution.py:18
  214.3 2.0 constant_dynamic-update-slice_fusion.2
  216.3 6.1 %fusion.45 = f32[2,600]{1,0:T(2,128)S(1)} fusion(f32[3,2,600]{2,1,0:T(2,128)S(1)} %get-tuple-element.331, f32[3,600,600]{2,1,0:T(8,128)} %get-tuple-element.341, f32[16,2,600]{2,1,0:T(2,128)S(1)} %get-tuple-element.340, s32[]{:T(128)} %get-tuple-element.330), kind=kOutput, calls=%fused_computation.2.clone.1 | convolution fusion | flops 25921200 | bytes 4344004 | tf_op jit(solution)/shard_map/while/body/eval_jaxpr/cond/branch_1_fun/while/body/eval_jaxpr/jsn,jmn->sm/dot_general | solution.py:18
  222.5 2.0 constant_dynamic-update-slice_fusion.2
  224.5 6.1 %fusion.45 = f32[2,600]{1,0:T(2,128)S(1)} fusion(f32[3,2,600]{2,1,0:T(2,128)S(1)} %get-tuple-element.331, f32[3,600,600]{2,1,0:T(8,128)} %get-tuple-element.341, f32[16,2,600]{2,1,0:T(2,128)S(1)} %get-tuple-element.340, s32[]{:T(128)} %get-tuple-element.330), kind=kOutput, calls=%fused_computation.2.clone.1 | convolution fusion | flops 25921200 | bytes 4344004 | tf_op jit(solution)/shard_map/while/body/eval_jaxpr/cond/branch_1_fun/while/body/eval_jaxpr/jsn,jmn->sm/dot_general | solution.py:18
  230.7 2.0 constant_dynamic-update-slice_fusion.2
  232.7 1.3 collective-permute-start
  234.0 1.4 collective-permute-done
  235.4 1.5 copy.10
  237.0 169.9 %all-gather.2.cloned.1.call-done = f32[32,16,600]{2,1,0:T(8,128)} async-done(((f32[2,16,600]{2,1,0:T(8,128)}), f32[32,16,600]{2,1,0:T(8,128)}) %all-gather.2.cloned.1.call-update) | async-done | bytes 1228816 | tf_op jit(solution)/shard_map/all_gather | solution.py:61
  406.8 2.5 copy.47
  (60 shorter events, 5.8 us)
Async XLA Ops:
  6.5 21.2 %copy-start.1 = (bf16[32,16,512]{2,1,0:T(8,128)(2,1)S(1)}, bf16[32,16,512]{2,1,0:T(8,128)(2,1)}, u32[]{:S(2)}) copy-start(bf16[32,16,512]{2,1,0:T(8,128)(2,1)} %param.12) | copy-start | bytes 1572868
  6.5 88.6 %reduce-scatter.2.cloned.1.call-start = ((), (), s32[]{:S(2)}) async-start(), calls=%async_computation.1 | async-start | bytes 1392640 | tf_op jit(solution)/shard_map/reduce_scatter | solution.py:42
  7.8 16.9 %collective-permute-start.1 = (bf16[32,11,512]{2,1,0:T(8,128)(2,1)S(1)}, bf16[32,11,512]{2,1,0:T(8,128)(2,1)S(1)}, u32[]{:S(2)}, u32[]{:S(2)}) collective-permute-start(bf16[32,11,512]{2,1,0:T(8,128)(2,1)S(1)} %slice.30), channel_id=1, source_target_pairs={{0,1},{2,3},{4,5},{6,7},{8,9},{10,11},{12,13},{14,15},{16,17},{18,... | collective-permute-start | bytes 1081352 | tf_op jit(solution)/shard_map/ppermute | solution.py:12
  24.7 5.8 %slice-start = ((s8[4915200]{0:T(1024)(128)(4,1)}), s8[4194304]{0:T(1024)(128)(4,1)S(1)}, s32[]{:S(2)}) async-start(s8[4915200]{0:T(1024)(128)(4,1)} %bitcast.84), calls=%async_computation.3 | async-start | bytes 8388608
  28.2 2.2 slice-start.1
  30.4 66.3 %copy-start = (f32[600,600]{1,0:T(8,128)S(1)}, f32[600,600]{1,0:T(8,128)}, u32[]{:S(2)}) copy-start(f32[600,600]{1,0:T(8,128)} %param.16) | copy-start | bytes 4320004
  35.0 371.9 %all-gather.2.cloned.1.call-start = ((), (), s32[]{:S(2)}) async-start(), calls=%async_computation.2 | async-start | bytes 1392640 | tf_op jit(solution)/shard_map/all_gather | solution.py:61
  96.7 4.8 %collective-permute-start = (f32[3,2,600]{2,1,0:T(2,128)S(1)}, f32[3,2,600]{2,1,0:T(2,128)S(1)}, u32[]{:S(2)}, u32[]{:S(2)}) collective-permute-start(f32[3,2,600]{2,1,0:T(2,128)S(1)} %get-tuple-element.358), channel_id=1, source_target_pairs={{0,1},{2,3},{4,5},{6,7},{8,9},{10,11},{12,13},{14,15},{16,17},{18,... | collective-permute-start | bytes 43208 | tf_op jit(solution)/shard_map/while/body/eval_jaxpr/ppermute | solution.py:12
  232.7 2.7 collective-permute-start
Sparse Core Ops, SparseCore 0:
  35.1 59.9 reduce-scatter.1
  237.1 169.6 all-gather.1
where the time goes:
time: 417 us; the launch traced here: 416 us
  waiting for transfers between devices  233 us (56%)
  matrix products  135 us (32%)
  between operations  23.8 us (6%)
  starting transfers between devices  9.59 us (2%)
  local copies, waits for them, and re-layouts  7.62 us (2%)
  other arithmetic  6.76 us (2%)
    all_gather x1, waiting for transfers between devices, per_device(): return lax.all_gather(outputs, 'param', axis=0, tiled=True)  170 us
    dot_general x16, matrix products, advance(): jnp.einsum('jsn,jmn->sm', history, coupling, precision=lax.Precision.HIGH...  98.3 us
    reduce_scatter x1, waiting for transfers between devices, per_device(): summed = lax.psum_scatter(local, 'param', scatter_dimension=0, tiled=True)  60.1 us
    dot_general x16, matrix products, advance(): solved = jnp.dot(balance, diag_inverse.T, precision=lax.Precision.HIGHEST)  32.4 us
    ppermute x3, starting transfers between devices, from_behind(): return lax.ppermute(block, axis, route)  9.54 us
  transfers between devices with their start and end apart: 5, of which 4 were waited for; matrix products, arithmetic and copies ran while one was open for 0% of the time, Pallas kernels for 0%

commit v1 on v0

v1 whole, which is shorter than its diff:
```python
import functools
import jax
import jax.numpy as jnp
from jax import lax
from jax.experimental import pallas as pl
from jax.experimental.pallas import tpu as pltpu
from jax.sharding import PartitionSpec as P

REACH = 12
LANES = 128
ROWS = 8


def from_behind(block, axis, distance):
    devices = range(lax.axis_size(axis))
    route = [(i - distance, i) for i in devices if i - distance in devices]
    return lax.ppermute(block, axis, route)


def halves(value):
    high = value.astype(jnp.bfloat16).astype(jnp.float32)
    return jnp.concatenate([high, value - high], axis=0).astype(jnp.bfloat16)


def chain_kernel(band, base_ref, weights_ref, out_ref):
    steps, rows, width = base_ref.shape

    def advance(step, past):
        product = jnp.dot(
            jnp.concatenate(past, axis=-1), weights_ref[...], preferred_element_type=jnp.float32
        )
        solved = base_ref[step] - (
            product[:rows, :width] + product[rows:, :width] + product[:rows, width:]
        )
        out_ref[step] = solved
        return (halves(solved),) + past[:-1]

    nothing = halves(base_ref[0] * 0.0)
    lax.fori_loop(0, steps, advance, (nothing,) * band)


def per_device(params, kernel, lag_offsets, observed, diag_inverse, coupling):
    samples, step_count, col_count = params.shape
    lag_count, unused_cols, sensors = kernel.shape
    band = coupling.shape[0]
    width = -(-sensors // LANES) * LANES
    extra = width - sensors
    flat_kernel = kernel.reshape(lag_count * col_count, sensors)
    rim = from_behind(params[:, step_count - (REACH - 1) :, :], "tm", 1)
    source = jnp.concatenate([rim, params], axis=1)
    windows = [
        lax.dynamic_slice_in_dim(source, REACH - 1 - lag_offsets[lag_index], step_count, 1)
        for lag_index in range(lag_count)
    ]
    stacked = jnp.stack(windows, axis=2).reshape(samples * step_count, lag_count * col_count)
    product = jnp.dot(stacked, flat_kernel, preferred_element_type=jnp.float32)
    local = product.reshape(samples, step_count, sensors)
    summed = lax.psum_scatter(local, "param", scatter_dimension=0, tiled=True)
    share = summed.shape[0]
    mine = lax.dynamic_slice_in_dim(observed, lax.axis_index("param") * share, share, 0)
    misfit = mine.astype(jnp.float32) - summed

    weights = jnp.einsum("jkn,mk->jnm", coupling, diag_inverse, precision=lax.Precision.HIGHEST)
    weights = jnp.pad(weights, ((0, 0), (0, extra), (0, extra))).reshape(band * width, width)
    high = lax.reduce_precision(weights, 8, 7)
    pair = jnp.concatenate([high, weights - high], axis=-1).astype(jnp.bfloat16)

    base = jnp.dot(misfit, diag_inverse.T, precision=lax.Precision.HIGHEST)
    base = lax.all_gather(base, "tm", axis=1, tiled=True)
    total = base.shape[1]
    base = jnp.pad(jnp.swapaxes(base, 0, 1), ((0, 0), (0, ROWS - share), (0, extra)))
    solved = pl.pallas_call(
        functools.partial(chain_kernel, band),
        out_shape=jax.ShapeDtypeStruct((total, ROWS, width), jnp.float32),
        in_specs=[pl.BlockSpec(memory_space=pltpu.VMEM)] * 2,
        out_specs=pl.BlockSpec(memory_space=pltpu.VMEM),
    )(base, pair)
    own = lax.dynamic_slice_in_dim(solved, lax.axis_index("tm") * step_count, step_count, 0)
    outputs = jnp.swapaxes(own[:, :share, :sensors], 0, 1)
    return lax.all_gather(outputs, "param", axis=0, tiled=True)


def solution(mesh):
    in_specs = (P(None, "tm", "param"), P(None, "param", None), P(), P(None, "tm", None), P(), P())
    out_specs = P(None, "tm", None)
    return jax.shard_map(
        per_device, mesh=mesh, in_specs=in_specs, out_specs=out_specs, check_vma=False
    )
```

time: 417 us -> 181 us (0.43)
  waiting for transfers between devices: 233 us -> 67.4 us
  matrix products: 135 us -> 33.3 us
  Pallas kernels: 0 us -> 28 us
  blocking collectives: 0 us -> 5.11 us
  starting transfers between devices: 9.59 us -> 5.13 us
    all_gather x1, waiting for transfers between devices: 170 us -> 37.8 us  [per_device(): return lax.all_gather(outputs, 'param', axis=0, tiled=True)]
    dot_general x32 -> x2, matrix products: 131 us -> 28.9 us  [the longest x1 26.5 us: per_device(): jnp.einsum('jkn,mk->jnm', coupling, diag_inverse, precision=lax.Precision...]
    reduce_scatter x1, waiting for transfers between devices: 60.1 us -> 29.6 us  [per_device(): summed = lax.psum_scatter(local, 'param', scatter_dimension=0, tiled=True)]
    pallas_call x0 -> x1, Pallas kernels: none -> 28 us  [per_device(): pl.pallas_call(functools.partial(chain_kernel, band), out_shape=jax.Shape...]
    all_gather x0 -> x1, blocking collectives: none -> 5.11 us  [per_device(): base = lax.all_gather(base, 'tm', axis=1, tiled=True)]
    ppermute x3 -> x1, starting transfers between devices: 9.54 us -> 4.9 us  [from_behind(): return lax.ppermute(block, axis, route)]
  transfers between devices with their start and end apart: 5 -> 3, of which waited for: 4 -> 2; matrix products, arithmetic and copies ran while one was open for 0% -> 18% of each run, Pallas kernels for 0% -> 0%
where the time goes in v1:
time: 181 us; the launch traced here: 180 us
  waiting for transfers between devices  67.4 us (37%)
  matrix products  33.3 us (18%)
  Pallas kernels  28 us (15%)
  between operations  23.7 us (13%)
  other arithmetic  9.36 us (5%)
  local copies, waits for them, and re-layouts  8.32 us (5%)
  starting transfers between devices  5.13 us (3%)
  blocking collectives  5.11 us (3%)
    all_gather x1, waiting for transfers between devices, per_device(): return lax.all_gather(outputs, 'param', axis=0, tiled=True)  37.8 us
    reduce_scatter x1, waiting for transfers between devices, per_device(): summed = lax.psum_scatter(local, 'param', scatter_dimension=0, tiled=True)  29.6 us
    pallas_call x1, Pallas kernels, per_device(): pl.pallas_call(functools.partial(chain_kernel, band), out_shape=jax.Shape...  28 us
    dot_general x1, matrix products, per_device(): jnp.einsum('jkn,mk->jnm', coupling, diag_inverse, precision=lax.Precision...  26.5 us
    unnamed x8, other arithmetic  5.31 us
    all_gather x1, blocking collectives, per_device(): base = lax.all_gather(base, 'tm', axis=1, tiled=True)  5.11 us
    ppermute x1, starting transfers between devices, from_behind(): return lax.ppermute(block, axis, route)  4.9 us
    dot_general x1, matrix products, per_device(): product = jnp.dot(stacked, flat_kernel, preferred_element_type=jnp.float32)  4.5 us
  transfers between devices with their start and end apart: 3, of which 2 were waited for; matrix products, arithmetic and copies ran while one was open for 18% of the time, Pallas kernels for 0%

profile of v1, /device:TPU:0, one launch (start us, length us, event | category | flops | bytes accessed | tf_op | source)
XLA Modules:
  0.0 180.4 jit_solution(3721652315085850610)
XLA Ops:
  6.5 0.0 copy-start
  6.5 0.0 copy-start.1
  6.5 0.0 reduce-scatter.2.cloned.1.call-start
  6.5 1.3 slice.30
  7.9 4.9 %collective-permute-start = (bf16[32,11,512]{2,1,0:T(8,128)(2,1)S(1)}, bf16[32,11,512]{2,1,0:T(8,128)(2,1)S(1)}, u32[]{:S(2)}, u32[]{:S(2)}) collective-permute-start(bf16[32,11,512]{2,1,0:T(8,128)(2,1)S(1)} %slice.30), channel_id=1, source_target_pairs={{0,1},{2,3},{4,5},{6,7},{8,9},{10,11},{12,13},{14,15},{16,17},{18,... | collective-permute-start | bytes 1081352 | tf_op jit(solution)/shard_map/ppermute | solution.py:17
  12.8 1.6 fusion.38
  24.6 0.0 collective-permute-done
  24.6 0.0 slice-start
  24.6 1.6 fusion.15
  26.3 1.5 fusion.18
  27.8 0.0 copy-done.1
  27.8 0.4 fusion.21
  28.2 0.0 slice-start.1
  28.2 0.4 fusion.24
  28.7 0.4 fusion.27
  29.1 0.4 fusion.30
  29.6 0.4 fusion.33
  30.0 0.4 fusion.12
  30.4 0.0 slice-done
  30.4 0.0 slice-done.1
  30.4 4.5 %fusion.7 = f32[32,16,600]{2,1,0:T(8,128)} fusion(bf16[32,16,8,512]{3,1,0,2:T(8,128)(2,1)S(1)} %fusion.12, bf16[8,512,600]{1,2,0:T(8,128)(2,1)S(1)} %bitcast.72), kind=kOutput, calls=%fused_computation.26 | convolution fusion | flops 2516582400 | bytes 10338304 | tf_op jit(solution)/shard_map/dot_general | solution.py:56
  34.9 0.0 reduce-scatter.2.cloned.1.call-update
  35.0 0.2 all-gather.2.cloned.1.call-start
  35.2 0.0 copy-done
  35.2 26.5 %fusion.3 = f32[3,600,600]{2,1,0:T(8,128)S(1)} fusion(f32[3,600,600]{2,1,0:T(8,128)} %param.11, f32[600,600]{1,0:T(8,128)S(1)} %copy-done), kind=kOutput, calls=%fused_computation.22 | convolution fusion | flops 7776000000 | bytes 10080000 | tf_op jit(solution)/shard_map/jkn,mk->jnm/dot_general | solution.py:63
  61.7 0.3 pad.9
  62.0 1.1 reduce-precision_convert_fusion
  63.1 2.6 %pad_maximum_fusion.weights_ref = bf16[1920,1280]{1,0:T(8,128)(2,1)} fusion(bf16[1920,640]{1,0:T(8,128)(2,1)S(1)} %get-tuple-element.6, bf16[1920,640]{1,0:T(8,128)(2,1)S(1)} %get-tuple-element.5), kind=kLoop, calls=%fused_computation.3 | loop fusion | flops 9830400 | bytes 9830400 | tf_op jit(solution)/shard_map/concatenate | solution.py:66
  65.7 29.6 %reduce-scatter.2.cloned.1.call-done = f32[2,16,600]{2,1,0:T(8,128)} async-done(((f32[32,16,600]{2,1,0:T(8,128)}), f32[2,16,600]{2,1,0:T(8,128)}) %reduce-scatter.2.cloned.1.call-update) | async-done | bytes 76816 | tf_op jit(solution)/shard_map/reduce_scatter | solution.py:58
  95.3 2.3 %fusion.5 = f32[2,16,600]{2,1,0:T(8,128)S(1)} fusion(f32[600,600]{1,0:T(8,128)S(1)} %copy-done, f32[2,16,600]{2,1,0:T(8,128)} %reduce-scatter.2.cloned.1.call-done, bf16[32,16,600]{2,1,0:T(8,128)(2,1)} %param.9, s32[]{:T(128)S(6)} %select_n.30), kind=kOutput, calls=%fused_computation.24 | convolution fusion | flops 138278400 | bytes 1639684 | tf_op jit(solution)/shard_map/dot_general | solution.py:68
  97.7 5.1 %all_gather.6 = f32[2,32,600]{2,0,1:T(2,128)S(1)} all-gather(f32[2,16,600]{2,0,1:T(2,128)S(1)} %copy.10), channel_id=1, replica_groups=mesh['param'=16,'tm'=2] {'tm'}, dimensions={1}, use_global_device_ids=true | all-gather | bytes 230400 | tf_op jit(solution)/shard_map/all_gather | solution.py:69
  102.8 0.9 pad.8.base_ref
  103.7 28.0 %shard_map.64 = f32[32,8,640]{2,1,0:T(8,128)} custom-call(f32[32,8,640]{2,1,0:T(8,128)} %pad.8.base_ref, bf16[1920,1280]{1,0:T(8,128)(2,1)} %pad_maximum_fusion.weights_ref), custom_call_target="tpu_custom_call" | custom-call | tf_op jit(solution)/shard_map/pallas_call | solution.py:72
  131.7 1.0 dynamic-slice_bitcast_fusion
  132.7 0.6 copy.12
  133.3 0.0 all-gather.2.cloned.1.call-update
  133.3 37.8 %all-gather.2.cloned.1.call-done = f32[32,16,600]{2,1,0:T(8,128)} async-done(((f32[2,16,600]{2,1,0:T(8,128)}), f32[32,16,600]{2,1,0:T(8,128)}) %all-gather.2.cloned.1.call-update) | async-done | bytes 1228816 | tf_op jit(solution)/shard_map/all_gather | solution.py:80
  171.1 2.5 %copy.23 = f32[32,16,600]{2,1,0:T(8,128)} copy(f32[32,16,600]{2,1,0:T(8,128)} %all-gather.2.cloned.1.call-done) | data formatting | bytes 2457600
  (2 shorter events, 0.0 us)
Async XLA Ops:
  6.5 28.7 %copy-start = (f32[600,600]{1,0:T(8,128)S(1)}, f32[600,600]{1,0:T(8,128)}, u32[]{:S(2)}) copy-start(f32[600,600]{1,0:T(8,128)} %param.10) | copy-start | bytes 4320004
  6.5 21.2 %copy-start.1 = (bf16[32,16,512]{2,1,0:T(8,128)(2,1)S(1)}, bf16[32,16,512]{2,1,0:T(8,128)(2,1)}, u32[]{:S(2)}) copy-start(bf16[32,16,512]{2,1,0:T(8,128)(2,1)} %param.6) | copy-start | bytes 1572868
  6.5 88.7 %reduce-scatter.2.cloned.1.call-start = ((), (), s32[]{:S(2)}) async-start(), calls=%async_computation.1 | async-start | bytes 1392640 | tf_op jit(solution)/shard_map/reduce_scatter | solution.py:58
  7.9 16.7 %collective-permute-start = (bf16[32,11,512]{2,1,0:T(8,128)(2,1)S(1)}, bf16[32,11,512]{2,1,0:T(8,128)(2,1)S(1)}, u32[]{:S(2)}, u32[]{:S(2)}) collective-permute-start(bf16[32,11,512]{2,1,0:T(8,128)(2,1)S(1)} %slice.30), channel_id=1, source_target_pairs={{0,1},{2,3},{4,5},{6,7},{8,9},{10,11},{12,13},{14,15},{16,17},{18,... | collective-permute-start | bytes 1081352 | tf_op jit(solution)/shard_map/ppermute | solution.py:17
  24.6 5.8 %slice-start = ((s8[4915200]{0:T(1024)(128)(4,1)}), s8[4194304]{0:T(1024)(128)(4,1)S(1)}, s32[]{:S(2)}) async-start(s8[4915200]{0:T(1024)(128)(4,1)} %bitcast.71), calls=%async_computation.3 | async-start | bytes 8388608
  28.2 2.2 %slice-start.1 = ((s8[4915200]{0:T(1024)(128)(4,1)}), s8[720896]{0:T(1024)(128)(4,1)S(1)}, s32[]{:S(2)}) async-start(s8[4915200]{0:T(1024)(128)(4,1)} %bitcast.71), calls=%async_computation.4 | async-start | bytes 1441792
  35.0 136.1 %all-gather.2.cloned.1.call-start = ((), (), s32[]{:S(2)}) async-start(), calls=%async_computation.2 | async-start | bytes 1392640 | tf_op jit(solution)/shard_map/all_gather | solution.py:80
Sparse Core Ops, SparseCore 0:
  35.1 60.1 reduce-scatter.1
  133.5 37.6 all-gather.1

commit v2 on v1

--- a/solution.py
+++ b/solution.py
@@ -37,6 +37,124 @@
 
     nothing = halves(base_ref[0] * 0.0)
     lax.fori_loop(0, steps, advance, (nothing,) * band)
+
+
+MESH = pl.DeviceIdType.MESH
+
+
+def place():
+    me = lax.axis_index("param")
+    return lax.div(me, 2), lax.rem(me, 2), lax.axis_size("param") // 2
+
+
+def greet(chip, core, chips):
+    barrier = pltpu.get_barrier_semaphore()
+    others = [2 * chip + 1 - core]
+    others += [2 * lax.rem(chip + k, chips) + core for k in range(1, chips)]
+    for other in others:
+        pl.semaphore_signal(barrier, inc=1, device_id={"param": other}, device_id_type=MESH)
+    pl.semaphore_wait(barrier, chips)
+
+
+def send(source, target, send_sem, recv_sem, other):
+    copy = pltpu.make_async_remote_copy(
+        src_ref=source,
+        dst_ref=target,
+        send_sem=send_sem,
+        recv_sem=recv_sem,
+        device_id={"param": other},
+        device_id_type=MESH,
+    )
+    copy.start()
+    return copy
+
+
+def reduce_kernel(
+    local_ref, out_ref, pair_in, partial, landed, pair_send, pair_recv, chip_send, chip_recv
+):
+    chip, core, chips = place()
+    greet(chip, core, chips)
+    turns = [lax.rem(chip + k, chips) for k in range(1, chips + 1)]
+    pairs = [
+        send(local_ref.at[q, 1 - core], pair_in.at[k], pair_send.at[k], pair_recv.at[k], 2 * chip + 1 - core)
+        for k, q in enumerate(turns)
+    ]
+    sends = []
+    for k, q in enumerate(turns):
+        pairs[k].wait_recv()
+        if k < chips - 1:
+            partial[k] = local_ref[q, core] + pair_in[k]
+            sends.append(
+                send(partial.at[k], landed.at[k], chip_send.at[k], chip_recv.at[k], 2 * q + core)
+            )
+        else:
+            total = local_ref[q, core] + pair_in[k]
+    for k in range(chips - 1):
+        sends[k].wait_recv()
+        total = total + landed[k]
+    out_ref[...] = total
+    for copy in pairs + sends:
+        copy.wait_send()
+
+
+def gather_kernel(own_ref, out_ref, pair_send, pair_recv, chip_send, chip_recv):
+    chip, core, chips = place()
+    greet(chip, core, chips)
+    other = 2 * chip + 1 - core
+    sends = [
+        send(own_ref, out_ref.at[chip, core], chip_send.at[k - 1], chip_recv.at[k - 1], 2 * lax.rem(chip + k, chips) + core)
+        for k in range(1, chips)
+    ]
+    pairs = [send(own_ref, out_ref.at[chip, core], pair_send.at[0], pair_recv.at[0], other)]
+    out_ref[chip, core] = own_ref[...]
+    for k in range(1, chips):
+        sends[k - 1].wait_recv()
+        block = out_ref.at[lax.rem(chip - k + chips, chips), core]
+        pairs.append(send(block, block, pair_send.at[k], pair_recv.at[k], other))
+    for copy in pairs:
+        copy.wait_recv()
+    for copy in pairs + sends:
+        copy.wait_send()
+
+
+def reduce_scatter(local):
+    chips = lax.axis_size("param") // 2
+    share = local.shape[0] // (2 * chips)
+    block = (share,) + local.shape[1:]
+    return pl.pallas_call(
+        reduce_kernel,
+        out_shape=jax.ShapeDtypeStruct(block, jnp.float32),
+        in_specs=[pl.BlockSpec(memory_space=pltpu.VMEM)],
+        out_specs=pl.BlockSpec(memory_space=pltpu.VMEM),
+        scratch_shapes=[
+            pltpu.VMEM((chips,) + block, jnp.float32),
+            pltpu.VMEM((chips - 1,) + block, jnp.float32),
+            pltpu.VMEM((chips - 1,) + block, jnp.float32),
+            pltpu.SemaphoreType.DMA((chips,)),
+            pltpu.SemaphoreType.DMA((chips,)),
+            pltpu.SemaphoreType.DMA((chips - 1,)),
+            pltpu.SemaphoreType.DMA((chips - 1,)),
+        ],
+        compiler_params=pltpu.CompilerParams(collective_id=0, has_side_effects=True),
+    )(local.reshape((chips, 2) + block))
+
+
+def gather(own):
+    chips = lax.axis_size("param") // 2
+    whole = pl.pallas_call(
+        gather_kernel,
+        out_shape=jax.ShapeDtypeStruct((chips, 2) + own.shape, jnp.float32),
+        in_specs=[pl.BlockSpec(memory_space=pltpu.VMEM)],
+        out_specs=pl.BlockSpec(memory_space=pltpu.VMEM),
+        scratch_shapes=[
+            pltpu.SemaphoreType.DMA((chips,)),
+            pltpu.SemaphoreType.DMA((chips,)),
+            pltpu.SemaphoreType.DMA((chips - 1,)),
+            pltpu.SemaphoreType.DMA((chips - 1,)),
+        ],
+        compiler_params=pltpu.CompilerParams(collective_id=1, has_side_effects=True),
+    )(own)
+    return whole.reshape((2 * chips * own.shape[0],) + own.shape[1:])
 
 
 def per_device(params, kernel, lag_offsets, observed, diag_inverse, coupling):
@@ -55,12 +173,19 @@
     stacked = jnp.stack(windows, axis=2).reshape(samples * step_count, lag_count * col_count)
     product = jnp.dot(stacked, flat_kernel, preferred_element_type=jnp.float32)
     local = product.reshape(samples, step_count, sensors)
-    summed = lax.psum_scatter(local, "param", scatter_dimension=0, tiled=True)
+    summed = reduce_scatter(local)
     share = summed.shape[0]
     mine = lax.dynamic_slice_in_dim(observed, lax.axis_index("param") * share, share, 0)
     misfit = mine.astype(jnp.float32) - summed
 
-    weights = jnp.einsum("jkn,mk->jnm", coupling, diag_inverse, precision=lax.Precision.HIGHEST)
+    coupling_high = lax.reduce_precision(coupling, 8, 7)
+    inverse_high = lax.reduce_precision(diag_inverse, 8, 7)
+    weights = jnp.einsum(
+        "jkn,mk->jnm",
+        jnp.concatenate([coupling_high, coupling - coupling_high, coupling_high], axis=1).astype(jnp.bfloat16),
+        jnp.concatenate([inverse_high, inverse_high, diag_inverse - inverse_high], axis=1).astype(jnp.bfloat16),
+        preferred_element_type=jnp.float32,
+    )
     weights = jnp.pad(weights, ((0, 0), (0, extra), (0, extra))).reshape(band * width, width)
     high = lax.reduce_precision(weights, 8, 7)
     pair = jnp.concatenate([high, weights - high], axis=-1).astype(jnp.bfloat16)
@@ -77,7 +202,7 @@
     )(base, pair)
     own = lax.dynamic_slice_in_dim(solved, lax.axis_index("tm") * step_count, step_count, 0)
     outputs = jnp.swapaxes(own[:, :share, :sensors], 0, 1)
-    return lax.all_gather(outputs, "param", axis=0, tiled=True)
+    return gather(outputs)
 
 
 def solution(mesh):

time: 181 us -> 184 us (1.017); the launches traced: 180 us -> 181 us
  waiting for transfers between devices: 67.4 us -> 0.01 us
  local copies, waits for them, and re-layouts: 8.32 us -> 57.7 us
  Pallas kernels: 28 us -> 67.5 us
  matrix products: 33.3 us -> 19 us
  between operations: 23.7 us -> 10.1 us
  other arithmetic: 9.36 us -> 15.9 us
    pallas_call x0 -> x2, Pallas kernels: none -> 39.4 us  [the longest x1 21.4 us: gather(): pl.pallas_call(gather_kernel, out_shape=jax.ShapeDtypeStruct((chips, 2) +...]
    all_gather x1 -> x0, waiting for transfers between devices: 37.8 us -> none  [per_device(): return lax.all_gather(outputs, 'param', axis=0, tiled=True)]
    reduce_scatter x1 -> x0, waiting for transfers between devices: 29.6 us -> none  [per_device(): summed = lax.psum_scatter(local, 'param', scatter_dimension=0, tiled=True)]
    dot_general x1, matrix products: 26.5 us -> 8.36 us  [per_device(): jnp.einsum('jkn,mk->jnm', jnp.concatenate([coupling_high, coupling - coup...]
    concatenate x0 -> x2, local copies, waits for them, and re-layouts: none -> 15 us  [the longest x1 10.9 us: per_device(): jnp.concatenate([coupling_high, coupling - coupling_high, coupling_high],...]
    unnamed x9 -> x10, local copies, waits for them, and re-layouts: 2.48 us -> 15.4 us
    reshape x0 -> x1, local copies, waits for them, and re-layouts: none -> 8.58 us  [per_device(): flat_kernel = kernel.reshape(lag_count * col_count, sensors)]
    dot_general x0 -> x1, local copies, waits for them, and re-layouts: none -> 7.45 us  [per_device(): product = jnp.dot(stacked, flat_kernel, preferred_element_type=jnp.float32)]
  transfers between devices with their start and end apart: 3 -> 1, of which waited for: 2 -> 0; matrix products, arithmetic and copies ran while one was open for 18% -> 32% of each run, Pallas kernels for 0% -> 0%
where the time goes in v2:
time: 184 us; the launch traced here: 181 us
  Pallas kernels  67.5 us (37%)
  local copies, waits for them, and re-layouts  57.7 us (31%)
  matrix products  19 us (10%)
  other arithmetic  15.9 us (9%)
  between operations  10.1 us (5%)
  blocking collectives  5.69 us (3%)
  starting transfers between devices  4.9 us (3%)
    pallas_call x1, Pallas kernels, per_device(): pl.pallas_call(functools.partial(chain_kernel, band), out_shape=jax.Shape...  28 us
    pallas_call x1, Pallas kernels, gather(): pl.pallas_call(gather_kernel, out_shape=jax.ShapeDtypeStruct((chips, 2) +...  21.4 us
    pallas_call x1, Pallas kernels, reduce_scatter(): pl.pallas_call(reduce_kernel, out_shape=jax.ShapeDtypeStruct(block, jnp.f...  18 us
    unnamed x10, local copies, waits for them, and re-layouts  15.4 us
    concatenate x1, local copies, waits for them, and re-layouts, per_device(): jnp.concatenate([coupling_high, coupling - coupling_high, coupling_high],...  10.9 us
    reshape x1, local copies, waits for them, and re-layouts, per_device(): flat_kernel = kernel.reshape(lag_count * col_count, sensors)  8.58 us
    dot_general x1, matrix products, per_device(): jnp.einsum('jkn,mk->jnm', jnp.concatenate([coupling_high, coupling - coup...  8.36 us
    dot_general x1, matrix products, per_device(): product = jnp.dot(stacked, flat_kernel, preferred_element_type=jnp.float32)  8.27 us
  transfers between devices with their start and end apart: 1, of which 0 were waited for; matrix products, arithmetic and copies ran while one was open for 32% of the time, Pallas kernels for 0%

profile of v2, /device:TPU:0, one launch (start us, length us, event | category | flops | bytes accessed | tf_op | source)
XLA Modules:
  0.0 180.7 jit_solution(6741141059380610348)
XLA Ops:
  0.0 1.2 slice.30
  1.2 4.9 %collective-permute-start = (bf16[32,11,512]{2,1,0:T(8,128)(2,1)S(1)}, bf16[32,11,512]{2,1,0:T(8,128)(2,1)S(1)}, u32[]{:S(2)}, u32[]{:S(2)}) collective-permute-start(bf16[32,11,512]{2,1,0:T(8,128)(2,1)S(1)} %slice.30), channel_id=1, source_target_pairs={{0,1},{2,3},{4,5},{6,7},{8,9},{10,11},{12,13},{14,15},{16,17},{18,... | collective-permute-start | bytes 1081352 | tf_op jit(solution)/shard_map/ppermute | solution.py:17
  6.1 1.6 fusion.37
  17.7 6.3 %copy.23 = bf16[8,512,600]{1,0,2:T(8,128)(2,1)} copy(bf16[8,512,600]{1,2,0:T(8,128)(2,1)} %param.7) | data formatting | bytes 9830400 | tf_op args[1]
  24.0 8.6 %reshape.47 = bf16[4096,600,1,1,1]{0,1,2,3,4:T(8,128)(2,1)} reshape(bf16[8,512,600]{1,0,2:T(8,128)(2,1)} %copy.23) | data formatting | bytes 9830400 | tf_op jit(solution)/shard_map/reshape | solution.py:166
  32.5 6.0 %copy.25 = f32[3,600,600]{1,2,0:T(8,128)} copy(f32[3,600,600]{2,1,0:T(8,128)} %param.11) | data formatting | bytes 8640000 | tf_op args[5]
  38.6 0.0 copy-start.1
  38.6 4.6 %fusion.3 = (bf16[3,600,600]{1,2,0:T(8,128)(2,1)}, bf16[3,600,600]{1,2,0:T(8,128)(2,1)S(1)}) fusion(f32[3,600,600]{1,2,0:T(8,128)} %copy.25), kind=kLoop, calls=%fused_computation.8 | loop fusion | flops 4320000 | bytes 8640000 | tf_op jit(solution)/shard_map/convert.6
  43.1 0.0 copy-done.1
  43.1 1.4 fusion.6
  44.5 10.9 %concatenate.16 = bf16[3,1800,600]{1,2,0:T(8,128)(2,1)} concatenate(bf16[3,600,600]{1,2,0:T(8,128)(2,1)S(1)} %get-tuple-element.8, bf16[3,600,600]{1,2,0:T(8,128)(2,1)} %get-tuple-element.7, bf16[3,600,600]{1,2,0:T(8,128)(2,1)S(1)} %get-tuple-element.8), dimensions={1} | concatenate | bytes 12960000 | tf_op jit(solution)/shard_map/concatenate | solution.py:185
  55.4 4.0 %concatenate.17 = bf16[600,1800]{1,0:T(8,128)(2,1)S(1)} concatenate(bf16[600,600]{1,0:T(8,128)(2,1)} %get-tuple-element.10, bf16[600,600]{1,0:T(8,128)(2,1)} %get-tuple-element.10, bf16[600,600]{1,0:T(8,128)(2,1)} %get-tuple-element.9), dimensions={1} | concatenate | bytes 4320000 | tf_op jit(solution)/shard_map/concatenate | solution.py:186
  59.5 8.4 %fusion.4 = f32[3,600,600]{2,1,0:T(8,128)S(1)} fusion(bf16[3,1800,600]{1,2,0:T(8,128)(2,1)} %concatenate.16, bf16[600,1800]{1,0:T(8,128)(2,1)S(1)} %concatenate.17), kind=kOutput, calls=%fused_computation.9 | convolution fusion | flops 3888000000 | bytes 12960000 | tf_op jit(solution)/shard_map/jkn,mk->jnm/dot_general | solution.py:183
  67.8 0.3 pad.9
  68.2 2.3 %reduce-precision_convert_fusion = (bf16[1920,640]{1,0:T(8,128)(2,1)S(1)}, bf16[1920,640]{1,0:T(8,128)(2,1)}) fusion(f32[3,640,640]{2,1,0:T(8,128)S(1)} %pad.9), kind=kLoop, calls=%fused_computation.1 | loop fusion | flops 4915200 | bytes 9830400 | tf_op jit(solution)/shard_map/convert
  70.5 0.0 copy-start
  70.5 4.3 %pad_maximum_fusion.weights_ref = bf16[1920,1280]{1,0:T(8,128)(2,1)} fusion(bf16[1920,640]{1,0:T(8,128)(2,1)} %get-tuple-element.6, bf16[1920,640]{1,0:T(8,128)(2,1)S(1)} %get-tuple-element.5), kind=kLoop, calls=%fused_computation.5 | loop fusion | flops 9830400 | bytes 9830400 | tf_op jit(solution)/shard_map/concatenate | solution.py:191
  74.8 0.0 collective-permute-done
  74.8 0.0 copy-done
  74.8 0.4 fusion.14
  75.2 0.4 fusion.17
  75.6 0.4 fusion.20
  76.1 0.4 fusion.23
  76.5 0.4 fusion.26
  76.9 0.4 fusion.29
  77.3 0.4 fusion.32
  77.7 0.4 fusion.11
  78.2 6.2 %copy.22 = bf16[32,16,8,512]{3,2,1,0:T(8,128)(2,1)} copy(bf16[32,16,8,512]{3,1,0,2:T(8,128)(2,1)S(1)} %fusion.11) | data formatting | bytes 8388608 | tf_op jit(solution)/shard_map/stack | solution.py:173
  84.4 7.5 %dot_general.11 = bf16[8,2,2,16,4096]{4,3,2,1,0:T(8,128)(2,1)} reshape(bf16[32,16,8,512]{3,2,1,0:T(8,128)(2,1)} %copy.22) | data formatting | bytes 8388608 | tf_op jit(solution)/shard_map/dot_general | solution.py:174
  91.9 0.0 copy-start.2
  91.9 8.3 %fusion.1.local_ref = f32[8,2,2,16,600]{4,3,2,1,0:T(8,128)} fusion(bf16[8,2,2,16,4096]{4,3,2,1,0:T(8,128)(2,1)} %dot_general.11, bf16[4096,600,1,1,1]{0,1,2,3,4:T(8,128)(2,1)} %reshape.47), kind=kOutput, calls=%fused_computation.6 | convolution fusion | flops 2516582400 | bytes 10338304 | tf_op jit(solution)/shard_map/dot_general | solution.py:174
  100.1 18.0 %shard_map.64 = f32[2,16,600]{2,1,0:T(8,128)} custom-call(f32[8,2,2,16,600]{4,3,2,1,0:T(8,128)} %fusion.1.local_ref), custom_call_target="tpu_custom_call" | custom-call | tf_op jit(solution)/shard_map/pallas_call | solution.py:124
  118.2 0.0 copy-done.2
  118.2 2.4 %fusion.7 = f32[2,16,600]{2,1,0:T(8,128)S(1)} fusion(f32[600,600]{1,0:T(8,128)S(1)} %copy-done.2, f32[2,16,600]{2,1,0:T(8,128)} %shard_map.64, bf16[32,16,600]{2,1,0:T(8,128)(2,1)} %param.9, s32[]{:T(128)S(6)} %select_n.30), kind=kOutput, calls=%fused_computation.30 | convolution fusion | flops 138278400 | bytes 1639684 | tf_op jit(solution)/shard_map/dot_general | solution.py:193
  120.6 5.7 %all_gather.3 = f32[2,32,600]{2,0,1:T(2,128)S(1)} all-gather(f32[2,16,600]{2,0,1:T(2,128)S(1)} %copy.24), channel_id=1, replica_groups=mesh['param'=16,'tm'=2] {'tm'}, dimensions={1}, use_global_device_ids=true | all-gather | bytes 230400 | tf_op jit(solution)/shard_map/all_gather | solution.py:194
  126.3 0.9 pad.8.base_ref
  127.2 28.0 %shard_map.65 = f32[32,8,640]{2,1,0:T(8,128)} custom-call(f32[32,8,640]{2,1,0:T(8,128)} %pad.8.base_ref, bf16[1920,1280]{1,0:T(8,128)(2,1)} %pad_maximum_fusion.weights_ref), custom_call_target="tpu_custom_call" | custom-call | tf_op jit(solution)/shard_map/pallas_call | solution.py:197
  155.2 1.0 constant_dynamic-slice_fusion
  156.2 0.6 copy.32
  156.8 21.4 %shard_map.66 = f32[8,2,2,16,600]{4,3,2,1,0:T(8,128)} custom-call(f32[2,16,600]{2,1,0:T(8,128)} %bitcast.73), custom_call_target="tpu_custom_call" | custom-call | tf_op jit(solution)/shard_map/pallas_call | solution.py:144
  178.3 2.5 %copy.41 = f32[32,16,600]{2,1,0:T(8,128)} copy(f32[32,16,600]{2,1,0:T(8,128)} %bitcast.71) | data formatting | bytes 2457600
  (1 shorter events, 0.0 us)
Async XLA Ops:
  1.2 73.6 %collective-permute-start = (bf16[32,11,512]{2,1,0:T(8,128)(2,1)S(1)}, bf16[32,11,512]{2,1,0:T(8,128)(2,1)S(1)}, u32[]{:S(2)}, u32[]{:S(2)}) collective-permute-start(bf16[32,11,512]{2,1,0:T(8,128)(2,1)S(1)} %slice.30), channel_id=1, source_target_pairs={{0,1},{2,3},{4,5},{6,7},{8,9},{10,11},{12,13},{14,15},{16,17},{18,... | collective-permute-start | bytes 1081352 | tf_op jit(solution)/shard_map/ppermute | solution.py:17
  38.6 4.6 %copy-start.1 = (f32[600,600]{1,0:T(8,128)S(1)}, f32[600,600]{1,0:T(8,128)}, u32[]{:S(2)}) copy-start(f32[600,600]{1,0:T(8,128)} %param.10) | copy-start | bytes 4320004
  70.5 4.3 %copy-start = (bf16[32,16,512]{2,1,0:T(8,128)(2,1)S(1)}, bf16[32,16,512]{2,1,0:T(8,128)(2,1)}, u32[]{:S(2)}) copy-start(bf16[32,16,512]{2,1,0:T(8,128)(2,1)} %param.6) | copy-start | bytes 1572868
  91.9 26.3 %copy-start.2 = (f32[600,600]{1,0:T(8,128)S(1)}, f32[600,600]{1,0:T(8,128)}, u32[]{:S(2)}) copy-start(f32[600,600]{1,0:T(8,128)} %param.10) | copy-start | bytes 4320004

commit v3 on v2

--- a/solution.py
+++ b/solution.py
@@ -178,14 +178,7 @@
     mine = lax.dynamic_slice_in_dim(observed, lax.axis_index("param") * share, share, 0)
     misfit = mine.astype(jnp.float32) - summed
 
-    coupling_high = lax.reduce_precision(coupling, 8, 7)
-    inverse_high = lax.reduce_precision(diag_inverse, 8, 7)
-    weights = jnp.einsum(
-        "jkn,mk->jnm",
-        jnp.concatenate([coupling_high, coupling - coupling_high, coupling_high], axis=1).astype(jnp.bfloat16),
-        jnp.concatenate([inverse_high, inverse_high, diag_inverse - inverse_high], axis=1).astype(jnp.bfloat16),
-        preferred_element_type=jnp.float32,
-    )
+    weights = jnp.einsum("jkn,mk->jnm", coupling, diag_inverse, precision=lax.Precision.HIGH)
     weights = jnp.pad(weights, ((0, 0), (0, extra), (0, extra))).reshape(band * width, width)
     high = lax.reduce_precision(weights, 8, 7)
     pair = jnp.concatenate([high, weights - high], axis=-1).astype(jnp.bfloat16)

time: 184 us -> 165 us (0.90)
  local copies, waits for them, and re-layouts: 57.7 us -> 36.8 us
  matrix products: 19 us -> 24.8 us
  other arithmetic: 15.9 us -> 11.8 us
    concatenate x2 -> x0, local copies, waits for them, and re-layouts: 15 us -> none  [the longest x1 10.9 us: per_device(): jnp.concatenate([coupling_high, coupling - coupling_high, coupling_high],...]
    dot_general x1, matrix products: 8.36 us -> 14.3 us  [per_device(): jnp.einsum('jkn,mk->jnm', coupling, diag_inverse, precision=lax.Precision...]
    unnamed x10 -> x7, local copies, waits for them, and re-layouts: 15.4 us -> 9.44 us
    another operation x3 -> x1, other arithmetic: 8.25 us -> 3.29 us
  transfers between devices with their start and end apart: 1 -> 1, of which waited for: 0 -> 0; matrix products, arithmetic and copies ran while one was open for 32% -> 24% of each run, Pallas kernels for 0% -> 0%
where the time goes in v3:
time: 165 us; the launch traced here: 162 us
  Pallas kernels  67.5 us (41%)
  local copies, waits for them, and re-layouts  36.8 us (22%)
  matrix products  24.8 us (15%)
  other arithmetic  11.8 us (7%)
  between operations  10.2 us (6%)
  blocking collectives  5.69 us (3%)
  starting transfers between devices  4.9 us (3%)
    pallas_call x1, Pallas kernels, per_device(): pl.pallas_call(functools.partial(chain_kernel, band), out_shape=jax.Shape...  28 us
    pallas_call x1, Pallas kernels, gather(): pl.pallas_call(gather_kernel, out_shape=jax.ShapeDtypeStruct((chips, 2) +...  21.4 us
    pallas_call x1, Pallas kernels, reduce_scatter(): pl.pallas_call(reduce_kernel, out_shape=jax.ShapeDtypeStruct(block, jnp.f...  18 us
    dot_general x1, matrix products, per_device(): jnp.einsum('jkn,mk->jnm', coupling, diag_inverse, precision=lax.Precision...  14.3 us
    unnamed x7, local copies, waits for them, and re-layouts  9.44 us
    reshape x1, local copies, waits for them, and re-layouts, per_device(): flat_kernel = kernel.reshape(lag_count * col_count, sensors)  8.55 us
    dot_general x1, matrix products, per_device(): product = jnp.dot(stacked, flat_kernel, preferred_element_type=jnp.float32)  8.17 us
    dot_general x1, local copies, waits for them, and re-layouts, per_device(): product = jnp.dot(stacked, flat_kernel, preferred_element_type=jnp.float32)  7.39 us
  transfers between devices with their start and end apart: 1, of which 0 were waited for; matrix products, arithmetic and copies ran while one was open for 24% of the time, Pallas kernels for 0%

profile of v3, /device:TPU:0, one launch (start us, length us, event | category | flops | bytes accessed | tf_op | source)
XLA Modules:
  0.0 161.7 jit_solution(1890376183713406391)
XLA Ops:
  0.0 0.0 copy-start
  0.0 1.3 slice.30
  1.3 4.9 %collective-permute-start = (bf16[32,11,512]{2,1,0:T(8,128)(2,1)S(1)}, bf16[32,11,512]{2,1,0:T(8,128)(2,1)S(1)}, u32[]{:S(2)}, u32[]{:S(2)}) collective-permute-start(bf16[32,11,512]{2,1,0:T(8,128)(2,1)S(1)} %slice.30), channel_id=1, source_target_pairs={{0,1},{2,3},{4,5},{6,7},{8,9},{10,11},{12,13},{14,15},{16,17},{18,... | collective-permute-start | bytes 1081352 | tf_op jit(solution)/shard_map/ppermute | solution.py:17
  6.2 1.6 %fusion.35 = (s32[1]{0:T(128)}, s32[1]{0:T(128)}, s32[1]{0:T(128)}, s32[1]{0:T(128)}, s32[1]{0:T(128)}, /*index=5*/s32[1]{0:T(128)}, s32[1]{0:T(128)}, s32[1]{0:T(128)}) fusion(s32[8]{0:T(128)} %param.8), kind=kLoop, calls=%fused_computation.56 | loop fusion | bytes 64 | tf_op jit(solution)/shard_map/slice | solution.py:170
  17.9 6.3 %copy.20 = bf16[8,512,600]{1,0,2:T(8,128)(2,1)} copy(bf16[8,512,600]{1,2,0:T(8,128)(2,1)} %param.7) | data formatting | bytes 9830400 | tf_op args[1]
  24.3 8.5 %reshape.47 = bf16[4096,600,1,1,1]{0,1,2,3,4:T(8,128)(2,1)} reshape(bf16[8,512,600]{1,0,2:T(8,128)(2,1)} %copy.20) | data formatting | bytes 9830400 | tf_op jit(solution)/shard_map/reshape | solution.py:166
  32.8 0.0 copy-done
  32.8 14.3 %fusion.3 = f32[3,600,600]{2,1,0:T(8,128)S(1)} fusion(f32[3,600,600]{2,1,0:T(8,128)} %param.11, f32[600,600]{1,0:T(8,128)S(1)} %copy-done), kind=kOutput, calls=%fused_computation.22 | convolution fusion | flops 3888000000 | bytes 10080000 | tf_op jit(solution)/shard_map/jkn,mk->jnm/dot_general | solution.py:181
  47.1 0.3 pad.9
  47.5 3.3 %reduce-precision_convert_fusion = (bf16[1920,640]{1,0:T(8,128)(2,1)}, bf16[1920,640]{1,0:T(8,128)(2,1)}) fusion(f32[3,640,640]{2,1,0:T(8,128)S(1)} %pad.9), kind=kLoop, calls=%fused_computation.1 | loop fusion | flops 4915200 | bytes 9830400 | tf_op jit(solution)/shard_map/convert
  50.8 0.0 copy-start.1
  50.8 5.1 %pad_maximum_fusion.weights_ref = bf16[1920,1280]{1,0:T(8,128)(2,1)} fusion(bf16[1920,640]{1,0:T(8,128)(2,1)} %get-tuple-element.6, bf16[1920,640]{1,0:T(8,128)(2,1)} %get-tuple-element.5), kind=kLoop, calls=%fused_computation.3 | loop fusion | flops 9830400 | bytes 9830400 | tf_op jit(solution)/shard_map/concatenate | solution.py:184
  55.9 0.0 collective-permute-done
  55.9 0.0 copy-done.1
  55.9 0.4 fusion.12
  56.3 0.4 fusion.15
  56.7 0.4 fusion.18
  57.1 0.4 fusion.21
  57.6 0.4 fusion.24
  58.0 0.4 fusion.27
  58.4 0.4 fusion.30
  58.8 0.4 fusion.9
  59.3 6.3 %copy.19 = bf16[32,16,8,512]{3,2,1,0:T(8,128)(2,1)} copy(bf16[32,16,8,512]{3,1,0,2:T(8,128)(2,1)S(1)} %fusion.9) | data formatting | bytes 8388608 | tf_op jit(solution)/shard_map/stack | solution.py:173
  65.5 7.4 %dot_general.11 = bf16[8,2,2,16,4096]{4,3,2,1,0:T(8,128)(2,1)} reshape(bf16[32,16,8,512]{3,2,1,0:T(8,128)(2,1)} %copy.19) | data formatting | bytes 8388608 | tf_op jit(solution)/shard_map/dot_general | solution.py:174
  72.9 8.2 %fusion.1.local_ref = f32[8,2,2,16,600]{4,3,2,1,0:T(8,128)} fusion(bf16[8,2,2,16,4096]{4,3,2,1,0:T(8,128)(2,1)} %dot_general.11, bf16[4096,600,1,1,1]{0,1,2,3,4:T(8,128)(2,1)} %reshape.47), kind=kOutput, calls=%fused_computation.4 | convolution fusion | flops 2516582400 | bytes 10338304 | tf_op jit(solution)/shard_map/dot_general | solution.py:174
  81.1 18.0 %shard_map.64 = f32[2,16,600]{2,1,0:T(8,128)} custom-call(f32[8,2,2,16,600]{4,3,2,1,0:T(8,128)} %fusion.1.local_ref), custom_call_target="tpu_custom_call" | custom-call | tf_op jit(solution)/shard_map/pallas_call | solution.py:124
  99.1 2.4 %fusion.5 = f32[2,16,600]{2,1,0:T(8,128)S(1)} fusion(f32[600,600]{1,0:T(8,128)S(1)} %copy-done, f32[2,16,600]{2,1,0:T(8,128)} %shard_map.64, bf16[32,16,600]{2,1,0:T(8,128)(2,1)} %param.9, s32[]{:T(128)S(6)} %select_n.30), kind=kOutput, calls=%fused_computation.24 | convolution fusion | flops 138278400 | bytes 1639684 | tf_op jit(solution)/shard_map/dot_general | solution.py:186
  101.5 5.7 %all_gather.3 = f32[2,32,600]{2,0,1:T(2,128)S(1)} all-gather(f32[2,16,600]{2,0,1:T(2,128)S(1)} %copy.21), channel_id=1, replica_groups=mesh['param'=16,'tm'=2] {'tm'}, dimensions={1}, use_global_device_ids=true | all-gather | bytes 230400 | tf_op jit(solution)/shard_map/all_gather | solution.py:187
  107.2 0.9 pad.8.base_ref
  108.1 28.0 %shard_map.65 = f32[32,8,640]{2,1,0:T(8,128)} custom-call(f32[32,8,640]{2,1,0:T(8,128)} %pad.8.base_ref, bf16[1920,1280]{1,0:T(8,128)(2,1)} %pad_maximum_fusion.weights_ref), custom_call_target="tpu_custom_call" | custom-call | tf_op jit(solution)/shard_map/pallas_call | solution.py:190
  136.1 1.0 constant_dynamic-slice_fusion
  137.1 0.6 copy.29
  137.8 21.4 %shard_map.66 = f32[8,2,2,16,600]{4,3,2,1,0:T(8,128)} custom-call(f32[2,16,600]{2,1,0:T(8,128)} %bitcast.72), custom_call_target="tpu_custom_call" | custom-call | tf_op jit(solution)/shard_map/pallas_call | solution.py:144
  159.2 2.5 %copy.38 = f32[32,16,600]{2,1,0:T(8,128)} copy(f32[32,16,600]{2,1,0:T(8,128)} %bitcast.70) | data formatting | bytes 2457600
  (1 shorter events, 0.0 us)
Async XLA Ops:
  0.0 32.8 %copy-start = (f32[600,600]{1,0:T(8,128)S(1)}, f32[600,600]{1,0:T(8,128)}, u32[]{:S(2)}) copy-start(f32[600,600]{1,0:T(8,128)} %param.10) | copy-start | bytes 4320004
  1.3 54.5 %collective-permute-start = (bf16[32,11,512]{2,1,0:T(8,128)(2,1)S(1)}, bf16[32,11,512]{2,1,0:T(8,128)(2,1)S(1)}, u32[]{:S(2)}, u32[]{:S(2)}) collective-permute-start(bf16[32,11,512]{2,1,0:T(8,128)(2,1)S(1)} %slice.30), channel_id=1, source_target_pairs={{0,1},{2,3},{4,5},{6,7},{8,9},{10,11},{12,13},{14,15},{16,17},{18,... | collective-permute-start | bytes 1081352 | tf_op jit(solution)/shard_map/ppermute | solution.py:17
  50.8 5.1 %copy-start.1 = (bf16[32,16,512]{2,1,0:T(8,128)(2,1)S(1)}, bf16[32,16,512]{2,1,0:T(8,128)(2,1)}, u32[]{:S(2)}) copy-start(bf16[32,16,512]{2,1,0:T(8,128)(2,1)} %param.6) | copy-start | bytes 1572868
